TPU v7x, 128 devices: a whole 4x4x4 slice. The times are simulated.
128 devices in a mesh: batch: 4 (over y_lo, core), tensor: 8 (over x, y_hi), latent: 4 (over z).
Axes of the slice: x: 4, y: 4 (y_hi: 2, y_lo: 2; y = y_hi * 2 + y_lo), z: 4, core: 2. Of those that a mesh axis runs over, the one named last changes fastest.
Arguments:
- residual: bfloat16 [1024, 3584], P('batch', ('tensor', 'latent')), may hold values from -6 to 6
- target: bfloat16 [1024, 3584], P('batch', ('tensor', 'latent')), may hold values from -6 to 6
- encoder_weight: bfloat16 [3584, 32768], P(None, ('tensor', 'latent')), may hold values from -0.09375 to 0.09375
- encoder_bias: bfloat16 [32768], P(('tensor', 'latent')), may hold values from -0.59765625 to 0.29882812
- decoder_weight: bfloat16 [32768, 3584], P(('tensor', 'latent')), may hold values from -0.09375 to 0.09375
- decoder_bias: bfloat16 [3584], replicated, may hold values from -3 to 3
- first_gain: bfloat16 [3584], replicated, may hold values from 0.5 to 1.5
- second_gain: bfloat16 [3584], replicated, may hold values from 0.5 to 1.5
- gate_weight: bfloat16 [3584, 7168], P(None, ('tensor', 'latent')), may hold values from -0.09375 to 0.09375
- up_weight: bfloat16 [3584, 7168], P(None, ('tensor', 'latent')), may hold values from -0.09375 to 0.09375
- down_weight: bfloat16 [7168, 3584], P(('tensor', 'latent')), may hold values from -0.125 to 0.125
Outputs:
- encoder_grad: bfloat16 [3584, 32768], P('batch', ('tensor', 'latent'))
- decoder_grad: bfloat16 [32768, 3584], P(('tensor', 'latent'), 'batch')
All inputs are finite; a program needn't handle non-finite values.
Results may differ from a plain program's by a relative error of at most 0.012.
The roundings to bfloat16 on the way count: a program that leaves them out, or rounds other values in their place, can miss the bound.
Values may be sent and summed in bfloat16 or wider, within the bound.
No kernel may reach another device: no remote copies, remote signals or barrier semaphores. Data moves between devices by JAX's collectives and lax.ppermute only.
A program may use at most 128 MiB of HBM per device.

v0:
```python
import jax
import jax.numpy as jnp
from jax import lax
from jax.sharding import Mesh
from jax.sharding import PartitionSpec as P

TENSOR_LATENT = ("tensor_0", "tensor_1", "latent")
epsilon = 1e-06


def rows_for(lines, count):
    spare = -len(lines) % count
    return jnp.pad(lines, [(0, spare)] + [(0, 0)] * (lines.ndim - 1))


def copy_for_each(shard, axis):
    copies = jnp.broadcast_to(shard, (lax.axis_size(axis), *shard.shape))
    return lax.all_to_all(copies, axis, split_axis=0, concat_axis=0, tiled=True)


def laid_out(pieces, dim):
    pieces = jnp.moveaxis(pieces, 0, dim)
    lengths = pieces.shape
    return pieces.reshape(*lengths[:dim], lengths[dim] * lengths[dim + 1], *lengths[dim + 2 :])


def whole_of(shard, axes, dim):
    far, near = axes
    initial = copy_for_each(shard, far)
    pieces = jnp.swapaxes(copy_for_each(initial, near), 0, 1)
    return laid_out(pieces.reshape(-1, *shard.shape), dim)


def split_up(shard, dim, count):
    lengths = shard.shape
    pieces = shard.reshape(*lengths[:dim], count, lengths[dim] // count, *lengths[dim + 1 :])
    return jnp.moveaxis(pieces, dim, 0)


def sum_at_owner(shard, axis, dim):
    pieces = split_up(shard, dim, lax.axis_size(axis))
    arrived = lax.all_to_all(pieces, axis, split_axis=0, concat_axis=0, tiled=True)
    return arrived.astype(jnp.float32).sum(axis=0)


def summed_rows(shard, axes, dim):
    far, near = axes
    own = sum_at_owner(split_up(shard, dim, lax.axis_size(far)), near, dim + 1)
    return jnp.sum(
        lax.all_to_all(own.astype(jnp.bfloat16), far, 0, 0, tiled=True).astype(jnp.float32), axis=0
    )


def total_of(shard, axes):
    lines = shard.reshape(-1, shard.shape[-1])
    padded = rows_for(lines, lax.axis_size(axes[0]) * lax.axis_size(axes[1]))
    whole = whole_of(summed_rows(padded, axes, 0).astype(jnp.bfloat16), axes, 0)
    return lax.slice_in_dim(whole, 0, len(lines)).reshape(shard.shape).astype(jnp.float32)


def sum_in_order(pieces, axes, order):
    inside = pieces.shape[1:]
    pieces = pieces.reshape(*(lax.axis_size(a) for a in axes), *inside)
    pieces = jnp.moveaxis(pieces, order, range(len(axes))).reshape(-1, *inside)
    for k in order:
        pieces = lax.psum_scatter(pieces, axes[k], scatter_dimension=0, tiled=True)
    return pieces[0]


def summed_rows_2(shard, axes, order, dim):
    count = lax.axis_size(axes)
    return sum_in_order(split_up(shard, dim, count), axes, order)


def over_copies(shard, axis):
    return copy_for_each(shard, axis).sum(axis=0)


def in_one_piece(arrays, axis, dim, along):
    both = jnp.concatenate(arrays, axis=along)
    out, at, gathered = (lax.all_gather(both, axis, axis=dim, tiled=True), 0, [])
    for a in arrays:
        gathered.append(lax.slice_in_dim(out, at, at + a.shape[along], axis=along))
        at += a.shape[along]
    return tuple(gathered)


def per_device(
    residual,
    target,
    encoder_weight,
    encoder_bias,
    decoder_weight,
    decoder_bias,
    first_gain,
    second_gain,
    gate_weight,
    up_weight,
    down_weight,
):
    f32 = jnp.float32
    bf16 = jnp.bfloat16
    contract_last = (((1,), (1,)), ((), ()))
    contract_first = (((0,), (0,)), ((), ()))
    share_width = residual.shape[1]
    model_width = share_width * lax.axis_size(TENSOR_LATENT)
    offset = lax.axis_index(TENSOR_LATENT) * share_width
    token_count = residual.shape[0] * lax.axis_size("batch")
    bias_share = lax.dynamic_slice_in_dim(decoder_bias.astype(f32), offset, share_width)
    first_share = lax.dynamic_slice_in_dim(first_gain.astype(f32), offset, share_width)
    second_share = lax.dynamic_slice_in_dim(second_gain.astype(f32), offset, share_width)
    centered_share = (residual.astype(f32) - bias_share).astype(bf16)
    centered = lax.all_gather(centered_share, TENSOR_LATENT, axis=1, tiled=True)
    preact = jnp.dot(centered, encoder_weight, preferred_element_type=f32) + encoder_bias.astype(
        f32
    )
    latents = jnp.maximum(preact, 0.0).astype(bf16)
    partial_recon = jnp.dot(latents, decoder_weight, preferred_element_type=f32)
    recon_full = total_of(
        partial_recon.astype(jnp.bfloat16), (("tensor_0", "tensor_1"), "latent")
    ) + decoder_bias.astype(f32)
    scale_in = lax.rsqrt(
        jnp.sum(recon_full * recon_full, axis=1, keepdims=True) / model_width + epsilon
    )
    normed_input = (recon_full * scale_in * first_gain.astype(f32)).astype(bf16)
    recon = lax.dynamic_slice_in_dim(recon_full, offset, share_width, 1)
    gate_value = jnp.dot(normed_input, gate_weight, preferred_element_type=f32)
    up_value = jnp.dot(normed_input, up_weight, preferred_element_type=f32)
    gelu_value, gelu_back = jax.vjp(lambda v: jax.nn.gelu(v, approximate=True), gate_value)
    hidden = (gelu_value * up_value).astype(bf16)
    partial_out = jnp.dot(hidden, down_weight, preferred_element_type=f32)
    output = summed_rows_2(partial_out.astype(jnp.bfloat16), TENSOR_LATENT, (0, 2, 1), 1).astype(
        jnp.float32
    )
    out_squares = over_copies(jnp.sum(output * output, axis=1), TENSOR_LATENT)
    scale_out = lax.rsqrt(out_squares[:, None] / model_width + epsilon)
    normed_out = output * scale_out
    result = recon + normed_out * second_share
    grad_result = 2.0 * (result - target.astype(f32)) / token_count
    grad_normed = grad_result * second_share
    inner_out = over_copies(jnp.sum(grad_normed * normed_out, axis=1), TENSOR_LATENT) / model_width
    grad_share = (scale_out * (grad_normed - normed_out * inner_out[:, None])).astype(bf16)
    grad_output = lax.all_gather(grad_share, TENSOR_LATENT, axis=1, tiled=True)
    grad_hidden = lax.dot_general(
        grad_output, down_weight, contract_last, preferred_element_type=f32
    )
    grad_gate = gelu_back(grad_hidden * up_value)[0].astype(bf16)
    grad_up = (grad_hidden * gelu_value).astype(bf16)
    partial_input = lax.dot_general(
        grad_gate, gate_weight, contract_last, preferred_element_type=f32
    )
    partial_input = partial_input + lax.dot_general(
        grad_up, up_weight, contract_last, preferred_element_type=f32
    )
    grad_normed_in = sum_at_owner(partial_input.astype(jnp.bfloat16), TENSOR_LATENT, 1)
    unit = recon * scale_in
    grad_unit = grad_normed_in * first_share
    inner_in = over_copies(jnp.sum(grad_unit * unit, axis=1), TENSOR_LATENT) / model_width
    recon_share = (grad_result + scale_in * (grad_unit - unit * inner_in[:, None])).astype(bf16)
    grad_recon = lax.all_gather(recon_share, TENSOR_LATENT, axis=1, tiled=True)
    grad_latent = lax.dot_general(
        grad_recon, decoder_weight, contract_last, preferred_element_type=f32
    )
    grad_preact = jnp.where(preact > 0, grad_latent, 0.0).astype(bf16)
    centered_block, recon_block = (
        lax.all_to_all(centered, "batch", split_axis=1, concat_axis=0, tiled=True),
        lax.all_to_all(grad_recon, "batch", split_axis=1, concat_axis=0, tiled=True),
    )
    latents_all, preact_all = in_one_piece((latents, grad_preact), "batch", 0, 1)
    encoder_grad = lax.dot_general(
        centered_block, preact_all, contract_first, preferred_element_type=f32
    )
    decoder_grad = lax.dot_general(
        latents_all, recon_block, contract_first, preferred_element_type=f32
    )
    return (encoder_grad.astype(bf16), decoder_grad.astype(bf16))


def solution(mesh):
    split = Mesh(
        mesh.devices.reshape(mesh.shape["batch"], 4, 2, mesh.shape["latent"]),
        ("batch", "tensor_0", "tensor_1", "latent"),
    )
    in_specs = (
        P("batch", TENSOR_LATENT),
        P("batch", TENSOR_LATENT),
        P(None, TENSOR_LATENT),
        P(TENSOR_LATENT),
        P(TENSOR_LATENT, None),
        P(),
        P(),
        P(),
        P(None, TENSOR_LATENT),
        P(None, TENSOR_LATENT),
        P(TENSOR_LATENT, None),
    )
    out_specs = (P("batch", TENSOR_LATENT), P(TENSOR_LATENT, "batch"))
    return jax.shard_map(
        per_device, mesh=split, in_specs=in_specs, out_specs=out_specs, check_vma=False
    )
```

profile of v0, /device:TPU:1, one launch (start us, length us, event | category | flops | bytes accessed | tf_op | source)
XLA Modules:
  0.0 584.4 jit_solution(9790143516048892075)
XLA Ops:
  10.3 72.6 %all-gather.5.cloned.1.call-done = bf16[256,3584]{0,1:T(8,128)(2,1)} async-done(((bf16[256,112]{0,1:T(8,128)(2,1)}), bf16[256,3584]{0,1:T(8,128)(2,1)}) %all-gather.5.cloned.1.call-update) | async-done | bytes 1835024 | tf_op jit(solution)/shard_map/all_gather | solution.py:113
  82.9 6.7 %maximum_convert_fusion = (bf16[256,1024]{1,0:T(8,128)(2,1)S(1)}, f32[256,1024]{1,0:T(8,128)}) fusion(f32[1024]{0:T(1024)S(1)} %convert_element_type.91, bf16[256,3584]{0,1:T(8,128)(2,1)} %all-gather.5.cloned.1.call-done, bf16[3584,1024]{1,0:T(8,128)(2,1)} %param.13), kind=kOutput, calls=%fused_computation.20 | convolution fusion | flops 1879834624 | bytes 10752000 | tf_op jit(solution)/shard_map/dot_general | solution.py:114
  89.7 5.3 convolution_convert_fusion
  95.2 23.6 %all_to_all.81 = bf16[4,8,8,3584]{3,2,1,0:T(8,128)(2,1)S(1)} all-to-all(bf16[4,8,8,3584]{3,2,1,0:T(8,128)(2,1)S(1)} %bitcast.58), channel_id=1, replica_groups=mesh['batch'=4,'tensor_0'=4,'tensor_1'=2,'latent'=4] {'latent'}, dimensions={0} | all-to-all | bytes 3670016 | tf_op jit(solution)/shard_map/all_to_all | solution.py:42
  119.9 11.9 %all_to_all.82 = bf16[8,8,3584]{2,1,0:T(8,128)(2,1)S(1)} all-to-all(bf16[8,8,3584]{2,1,0:T(8,128)(2,1)} %reduce_sum.98), channel_id=1, replica_groups=mesh['batch'=4,'tensor_0'=4,'tensor_1'=2,'latent'=4] {'tensor_0','tensor..., dimensions={0} | all-to-all | bytes 917504 | tf_op jit(solution)/shard_map/all_to_all | solution.py:50
  131.9 11.1 %all_to_all.83 = bf16[8,8,3584]{2,1,0:T(8,128)(2,1)S(1)} all-to-all(bf16[8,8,3584]{2,1,0:T(8,128)(2,1)S(1)} %broadcast_in_dim.11), channel_id=1, replica_groups=mesh['batch'=4,'tensor_0'=4,'tensor_1'=2,'latent'=4] {'tensor_0','tensor..., dimensions={0} | all-to-all | bytes 917504 | tf_op jit(solution)/shard_map/all_to_all | solution.py:18
  148.2 17.5 %all-to-all-done.4 = bf16[4,8,8,3584]{3,2,1,0:T(8,128)(2,1)S(1)} async-done(((bf16[4,8,8,3584]{3,2,1,0:T(8,128)(2,1)}), bf16[4,8,8,3584]{3,2,1,0:T(8,128)(2,1)S(1)}, u32[]{:S(2)}, u32[]{:S(2)}) %all-to-all-start.4) | async-done | bytes 1835040 | tf_op jit(solution)/shard_map/all_to_all | solution.py:18
  168.0 5.1 copy.51
  173.2 4.4 broadcast_add_fusion
  190.2 29.4 %reduce-scatter.4.cloned.1.call-done = bf16[8,256,112]{1,2,0:T(8,128)(2,1)} async-done(((bf16[32,256,112]{1,2,0:T(8,128)(2,1)}), bf16[8,256,112]{1,2,0:T(8,128)(2,1)}) %reduce-scatter.4.cloned.1.call-update) | async-done | bytes 458768 | tf_op jit(solution)/shard_map/reduce_scatter | solution.py:66
  219.7 21.8 %reduce-scatter.6.cloned.1.call-done = bf16[2,256,112]{1,2,0:T(8,128)(2,1)} async-done(((bf16[8,256,112]{1,2,0:T(8,128)(2,1)}), bf16[2,256,112]{1,2,0:T(8,128)(2,1)}) %reduce-scatter.6.cloned.1.call-update) | async-done | bytes 114704 | tf_op jit(solution)/shard_map/reduce_scatter | solution.py:66
  241.5 17.6 %reduce-scatter.8.cloned.1.call-done = bf16[1,256,112]{1,2,0:T(8,128)(2,1)} async-done(((bf16[2,256,112]{1,2,0:T(8,128)(2,1)}), bf16[1,256,112]{1,2,0:T(8,128)(2,1)}) %reduce-scatter.8.cloned.1.call-update) | async-done | bytes 57360 | tf_op jit(solution)/shard_map/reduce_scatter | solution.py:66
  260.5 7.0 %all-to-all-start.5 = ((f32[32,1,256]{2,1,0:T(1,128)}), f32[32,1,256]{2,1,0:T(1,128)S(1)}, u32[]{:S(2)}, u32[]{:S(2)}) async-start(f32[32,1,256]{2,1,0:T(1,128)} %broadcast_in_dim.13), calls=%async_computation.8 | async-start | bytes 65536 | tf_op jit(solution)/shard_map/all_to_all | solution.py:18
  268.3 7.9 %all-to-all-done.5 = f32[32,1,256]{2,1,0:T(1,128)S(1)} async-done(((f32[32,1,256]{2,1,0:T(1,128)}), f32[32,1,256]{2,1,0:T(1,128)S(1)}, u32[]{:S(2)}, u32[]{:S(2)}) %all-to-all-start.5) | async-done | bytes 32800 | tf_op jit(solution)/shard_map/all_to_all | solution.py:18
  277.4 12.1 %all_to_all.84 = f32[32,1,256]{2,1,0:T(1,128)S(1)} all-to-all(f32[32,1,256]{2,1,0:T(1,128)S(1)} %broadcast_in_dim.14), channel_id=1, replica_groups=mesh['batch'=4,'tensor_0'=4,'tensor_1'=2,'latent'=4] {'tensor_0','tensor..., dimensions={0} | all-to-all | bytes 65536 | tf_op jit(solution)/shard_map/all_to_all | solution.py:18
  291.2 66.7 %all-gather.7.cloned.1.call-done = bf16[256,3584]{0,1:T(8,128)(2,1)} async-done(((bf16[256,112]{0,1:T(8,128)(2,1)}), bf16[256,3584]{0,1:T(8,128)(2,1)}) %all-gather.7.cloned.1.call-update) | async-done | bytes 1835024 | tf_op jit(solution)/shard_map/all_gather | solution.py:143
  368.8 22.6 %all-to-all-done.7 = bf16[32,256,112]{1,2,0:T(8,128)(2,1)S(1)} async-done(((bf16[32,256,112]{1,2,0:T(8,128)(2,1)}), bf16[32,256,112]{1,2,0:T(8,128)(2,1)S(1)}, u32[]{:S(2)}, u32[]{:S(2)}) %all-to-all-start.7) | async-done | bytes 1835040 | tf_op jit(solution)/shard_map/all_to_all | solution.py:42
  392.6 16.3 %all_to_all.85 = f32[32,1,256]{2,1,0:T(1,128)S(1)} all-to-all(f32[32,1,256]{2,1,0:T(1,128)S(1)} %broadcast_in_dim.15), channel_id=1, replica_groups=mesh['batch'=4,'tensor_0'=4,'tensor_1'=2,'latent'=4] {'tensor_0','tensor..., dimensions={0} | all-to-all | bytes 65536 | tf_op jit(solution)/shard_map/all_to_all | solution.py:18
  410.6 66.5 %all-gather.9.cloned.1.call-done = bf16[256,3584]{0,1:T(8,128)(2,1)} async-done(((bf16[256,112]{0,1:T(8,128)(2,1)}), bf16[256,3584]{0,1:T(8,128)(2,1)}) %all-gather.9.cloned.1.call-update) | async-done | bytes 1835024 | tf_op jit(solution)/shard_map/all_gather | solution.py:160
  477.1 5.8 fusion.11
  484.8 44.0 %all_to_all.86 = bf16[256,4,896]{0,2,1:T(8,128)(2,1)} all-to-all(bf16[256,4,896]{0,2,1:T(8,128)(2,1)S(1)} %bitcast.54), channel_id=1, replica_groups=mesh['batch'=4,'tensor_0'=4,'tensor_1'=2,'latent'=4] {'batch'}, dimensions={1} | all-to-all | bytes 3670016 | tf_op jit(solution)/shard_map/all_to_all | solution.py:166
  528.8 5.0 all-to-all-start.9
  537.4 28.5 %all-to-all-done.9 = bf16[256,4,896]{0,2,1:T(8,128)(2,1)S(1)} async-done(((bf16[256,4,896]{0,2,1:T(8,128)(2,1)}), bf16[256,4,896]{0,2,1:T(8,128)(2,1)S(1)}, u32[]{:S(2)}, u32[]{:S(2)}) %all-to-all-start.9) | async-done | bytes 1835040 | tf_op jit(solution)/shard_map/all_to_all | solution.py:167
  568.3 5.9 %fusion.8 = bf16[1024,896]{1,0:T(8,128)(2,1)} fusion(bf16[1024,896]{1,0:T(8,128)(2,1)} %bitcast.62, bf16[1024,2048]{1,0:T(8,128)(2,1)} %all-gather.11.cloned.1.call-done), kind=kOutput, calls=%fused_computation.15 | convolution fusion | flops 1879965696 | bytes 5767168 | tf_op jit(solution)/shard_map/dot_general | solution.py:173
  (103 shorter events, 54.6 us)
Async XLA Ops:
  7.2 176.7 %copy-start = (bf16[224,3584]{1,0:T(8,128)(2,1)S(1)}, bf16[224,3584]{1,0:T(8,128)(2,1)}, u32[]{:S(2)}) copy-start(bf16[224,3584]{1,0:T(8,128)(2,1)} %param.21) | copy-start | bytes 4816900
  7.2 75.8 %all-gather.5.cloned.1.call-start = ((), (), s32[]{:S(2)}) async-start(), calls=%async_computation.13 | async-start | bytes 1892352 | tf_op jit(solution)/shard_map/all_gather | solution.py:113
  89.7 5.4 copy-start.10
  144.4 3.8 copy-start.18
  144.4 3.8 copy-start.19
  144.4 21.3 %all-to-all-start.4 = ((bf16[4,8,8,3584]{3,2,1,0:T(8,128)(2,1)}), bf16[4,8,8,3584]{3,2,1,0:T(8,128)(2,1)S(1)}, u32[]{:S(2)}, u32[]{:S(2)}) async-start(bf16[4,8,8,3584]{3,2,1,0:T(8,128)(2,1)} %broadcast_in_dim.12), calls=%async_computation.4 | async-start | bytes 3670016 | tf_op jit(solution)/shard_map/all_to_all | solution.py:18
  148.2 71.4 %reduce-scatter.4.cloned.1.call-start = ((), (), s32[]{:S(2)}) async-start(), calls=%async_computation.14 | async-start | bytes 2293760 | tf_op jit(solution)/shard_map/reduce_scatter | solution.py:66
  178.3 4.1 copy-start.5
  190.1 86.2 %copy-start.17 = (bf16[256,112]{0,1:T(8,128)(2,1)S(1)}, bf16[256,112]{0,1:T(8,128)(2,1)}, u32[]{:S(2)}) copy-start(bf16[256,112]{0,1:T(8,128)(2,1)} %param.12) | copy-start | bytes 172036
  190.1 51.3 %reduce-scatter.6.cloned.1.call-start = ((), (), s32[]{:S(2)}) async-start(), calls=%async_computation.15 | async-start | bytes 573440 | tf_op jit(solution)/shard_map/reduce_scatter | solution.py:66
  219.6 39.4 %reduce-scatter.8.cloned.1.call-start = ((), (), s32[]{:S(2)}) async-start(), calls=%async_computation.16 | async-start | bytes 172032 | tf_op jit(solution)/shard_map/reduce_scatter | solution.py:66
  260.5 15.7 %all-to-all-start.5 = ((f32[32,1,256]{2,1,0:T(1,128)}), f32[32,1,256]{2,1,0:T(1,128)S(1)}, u32[]{:S(2)}, u32[]{:S(2)}) async-start(f32[32,1,256]{2,1,0:T(1,128)} %broadcast_in_dim.13), calls=%async_computation.8 | async-start | bytes 65536 | tf_op jit(solution)/shard_map/all_to_all | solution.py:18
  267.5 90.4 %all-gather.7.cloned.1.call-start = ((), (), s32[]{:S(2)}) async-start(), calls=%async_computation.17 | async-start | bytes 1892352 | tf_op jit(solution)/shard_map/all_gather | solution.py:143
  291.2 68.8 %copy-start.4 = (bf16[3584,224]{0,1:T(8,128)(2,1)S(1)}, bf16[3584,224]{0,1:T(8,128)(2,1)}, u32[]{:S(2)}) copy-start(bf16[3584,224]{0,1:T(8,128)(2,1)} %param.19) | copy-start | bytes 4816900
  291.2 68.8 %copy-start.8 = (f32[256,224]{0,1:T(8,128)S(1)}, f32[256,224]{0,1:T(8,128)}, u32[]{:S(2)}) copy-start(f32[256,224]{0,1:T(8,128)} %copy-done.7) | copy-start | bytes 688132
  364.5 26.8 %all-to-all-start.7 = ((bf16[32,256,112]{1,2,0:T(8,128)(2,1)}), bf16[32,256,112]{1,2,0:T(8,128)(2,1)S(1)}, u32[]{:S(2)}, u32[]{:S(2)}) async-start(bf16[32,256,112]{1,2,0:T(8,128)(2,1)} %bitcast.16), calls=%async_computation.10 | async-start | bytes 3670016 | tf_op jit(solution)/shard_map/all_to_all | solution.py:42
  368.6 40.3 %copy-start.16 = (bf16[1,256,112]{1,2,0:T(8,128)(2,1)S(1)}, bf16[1,256,112]{1,2,0:T(8,128)(2,1)}, u32[]{:S(2)}) copy-start(bf16[1,256,112]{1,2,0:T(8,128)(2,1)} %reduce-scatter.8.cloned.1.call-done) | copy-start | bytes 172036
  368.6 108.5 %copy-start.15 = (f32[256,1024]{1,0:T(8,128)S(1)}, f32[256,1024]{1,0:T(8,128)}, u32[]{:S(2)}) copy-start(f32[256,1024]{1,0:T(8,128)} %get-tuple-element.5) | copy-start | bytes 3145732
  368.6 108.5 %all-gather.9.cloned.1.call-start = ((), (), s32[]{:S(2)}) async-start(), calls=%async_computation.18 | async-start | bytes 1892352 | tf_op jit(solution)/shard_map/all_gather | solution.py:160
  410.6 157.7 %all-gather.11.cloned.1.call-start = ((), (), s32[]{:S(2)}) async-start(), calls=%async_computation.19 | async-start | bytes 5242880 | tf_op jit(solution)/shard_map/all_gather | solution.py:81
  477.1 5.8 copy-start.11
  528.8 37.1 %all-to-all-start.9 = ((bf16[256,4,896]{0,2,1:T(8,128)(2,1)}), bf16[256,4,896]{0,2,1:T(8,128)(2,1)S(1)}, u32[]{:S(2)}, u32[]{:S(2)}) async-start(bf16[256,4,896]{0,2,1:T(8,128)(2,1)} %bitcast.60), calls=%async_computation.12 | async-start | bytes 3670016 | tf_op jit(solution)/shard_map/all_to_all | solution.py:167
  568.3 5.9 %copy-start.14 = (bf16[4,256,896]{2,1,0:T(8,128)(2,1)S(1)}, bf16[4,256,896]{2,1,0:T(8,128)(2,1)}, u32[]{:S(2)}) copy-start(bf16[4,256,896]{2,1,0:T(8,128)(2,1)} %copy.48) | copy-start | bytes 5505028
  568.3 5.9 %copy-start.20 = (bf16[1024,2048]{1,0:T(8,128)(2,1)S(1)}, bf16[1024,2048]{1,0:T(8,128)(2,1)}, u32[]{:S(2)}) copy-start(bf16[1024,2048]{1,0:T(8,128)(2,1)} %all-gather.11.cloned.1.call-done) | copy-start | bytes 12582916
  (8 other events, 15.3 us)
Sparse Core Ops, SparseCore 0:
  11.7 71.2 all-gather.4
  190.2 29.3 reduce-scatter.3
  222.0 19.4 reduce-scatter.5
  243.7 15.2 reduce-scatter.7
  291.3 66.5 all-gather.6
  410.7 66.3 all-gather.8
  484.2 72.1 all-gather.10
where the time goes:
time: 586 us; the launch traced here: 584 us
  waiting for transfers between devices  351 us (60%)
  blocking collectives  119 us (20%)
  matrix products  36.9 us (6%)
  local copies, waits for them, and re-layouts  23.7 us (4%)
  starting transfers between devices  20.1 us (3%)
  other arithmetic  19.1 us (3%)
  between operations  14.5 us (2%)
    all_gather x1, waiting for transfers between devices, per_device(): centered = lax.all_gather(centered_share, TENSOR_LATENT, axis=1, tiled=True)  72.6 us
    reduce_scatter x3, waiting for transfers between devices, sum_in_order(): pieces = lax.psum_scatter(pieces, axes[k], scatter_dimension=0, tiled=True)  68.8 us
    all_gather x1, waiting for transfers between devices, per_device(): grad_output = lax.all_gather(grad_share, TENSOR_LATENT, axis=1, tiled=True)  66.7 us
    all_gather x1, waiting for transfers between devices, per_device(): grad_recon = lax.all_gather(recon_share, TENSOR_LATENT, axis=1, tiled=True)  66.5 us
    all_to_all x1, blocking collectives, per_device(): lax.all_to_all(centered, 'batch', split_axis=1, concat_axis=0, tiled=True)  44 us
    all_to_all x3, blocking collectives, copy_for_each(): return lax.all_to_all(copies, axis, split_axis=0, concat_axis=0, tiled=True)  39.4 us
    all_to_all x1, waiting for transfers between devices, per_device(): lax.all_to_all(grad_recon, 'batch', split_axis=1, concat_axis=0, tiled=True)  28.5 us
    all_to_all x2, waiting for transfers between devices, copy_for_each(): return lax.all_to_all(copies, axis, split_axis=0, concat_axis=0, tiled=True)  25.4 us
  transfers between devices with their start and end apart: 11, of which 10 were waited for; matrix products, arithmetic and copies ran while one was open for 1% of the time, Pallas kernels for 0%

commit v1 on v0

--- a/solution.py
+++ b/solution.py
@@ -140,7 +140,10 @@
     grad_normed = grad_result * second_share
     inner_out = over_copies(jnp.sum(grad_normed * normed_out, axis=1), TENSOR_LATENT) / model_width
     grad_share = (scale_out * (grad_normed - normed_out * inner_out[:, None])).astype(bf16)
-    grad_output = lax.all_gather(grad_share, TENSOR_LATENT, axis=1, tiled=True)
+    grad_output = jnp.concatenate(
+        lax.all_to_all(jnp.stack([grad_share] * lax.axis_size(TENSOR_LATENT)), TENSOR_LATENT, 0, 0),
+        axis=1,
+    )
     grad_hidden = lax.dot_general(
         grad_output, down_weight, contract_last, preferred_element_type=f32
     )

time: 586 us -> 547 us (0.933)
  waiting for transfers between devices: 351 us -> 285 us
  blocking collectives: 119 us -> 145 us
    all_gather x1 -> x0, waiting for transfers between devices: 66.7 us -> none  [per_device(): grad_output = lax.all_gather(grad_share, TENSOR_LATENT, axis=1, tiled=True)]
    all_to_all x0 -> x1, blocking collectives: none -> 26.4 us  [per_device(): lax.all_to_all(jnp.stack([grad_share] * lax.axis_size(TENSOR_LATENT)), TE...]
  transfers between devices with their start and end apart: 11 -> 10, of which waited for: 10 -> 9; matrix products, arithmetic and copies ran while one was open for 1% -> 1% of each run, Pallas kernels for 0% -> 0%
where the time goes in v1:
time: 547 us; the launch traced here: 546 us
  waiting for transfers between devices  285 us (52%)
  blocking collectives  145 us (27%)
  matrix products  35.3 us (6%)
  local copies, waits for them, and re-layouts  24.7 us (5%)
  starting transfers between devices  23.3 us (4%)
  other arithmetic  18.5 us (3%)
  between operations  14.4 us (3%)
    all_gather x1, waiting for transfers between devices, per_device(): centered = lax.all_gather(centered_share, TENSOR_LATENT, axis=1, tiled=True)  72.6 us
    reduce_scatter x3, waiting for transfers between devices, sum_in_order(): pieces = lax.psum_scatter(pieces, axes[k], scatter_dimension=0, tiled=True)  68.8 us
    all_gather x1, waiting for transfers between devices, per_device(): grad_recon = lax.all_gather(recon_share, TENSOR_LATENT, axis=1, tiled=True)  65.9 us
    all_to_all x1, blocking collectives, per_device(): lax.all_to_all(centered, 'batch', split_axis=1, concat_axis=0, tiled=True)  44 us
    all_to_all x3, blocking collectives, copy_for_each(): return lax.all_to_all(copies, axis, split_axis=0, concat_axis=0, tiled=True)  38.8 us
    all_to_all x1, waiting for transfers between devices, per_device(): lax.all_to_all(grad_recon, 'batch', split_axis=1, concat_axis=0, tiled=True)  28.5 us
    all_to_all x1, blocking collectives, per_device(): lax.all_to_all(jnp.stack([grad_share] * lax.axis_size(TENSOR_LATENT)), TE...  26.4 us
    all_to_all x2, waiting for transfers between devices, copy_for_each(): return lax.all_to_all(copies, axis, split_axis=0, concat_axis=0, tiled=True)  25.5 us
  transfers between devices with their start and end apart: 10, of which 9 were waited for; matrix products, arithmetic and copies ran while one was open for 1% of the time, Pallas kernels for 0%

profile of v1, /device:TPU:1, one launch (start us, length us, event | category | flops | bytes accessed | tf_op | source)
XLA Modules:
  0.0 545.7 jit_solution(12142428231570238576)
XLA Ops:
  10.3 72.6 %all-gather.4.cloned.1.call-done = bf16[256,3584]{0,1:T(8,128)(2,1)} async-done(((bf16[256,112]{0,1:T(8,128)(2,1)}), bf16[256,3584]{0,1:T(8,128)(2,1)}) %all-gather.4.cloned.1.call-update) | async-done | bytes 1835024 | tf_op jit(solution)/shard_map/all_gather | solution.py:113
  82.9 6.7 %maximum_convert_fusion = (bf16[256,1024]{1,0:T(8,128)(2,1)S(1)}, f32[256,1024]{1,0:T(8,128)}) fusion(f32[1024]{0:T(1024)S(1)} %convert_element_type.91, bf16[256,3584]{0,1:T(8,128)(2,1)} %all-gather.4.cloned.1.call-done, bf16[3584,1024]{1,0:T(8,128)(2,1)} %param.13), kind=kOutput, calls=%fused_computation.20 | convolution fusion | flops 1879834624 | bytes 10752000 | tf_op jit(solution)/shard_map/dot_general | solution.py:114
  89.7 5.3 convolution_convert_fusion
  95.2 23.6 %all_to_all.86 = bf16[4,8,8,3584]{3,2,1,0:T(8,128)(2,1)S(1)} all-to-all(bf16[4,8,8,3584]{3,2,1,0:T(8,128)(2,1)S(1)} %bitcast.61), channel_id=1, replica_groups=mesh['batch'=4,'tensor_0'=4,'tensor_1'=2,'latent'=4] {'latent'}, dimensions={0} | all-to-all | bytes 3670016 | tf_op jit(solution)/shard_map/all_to_all | solution.py:42
  119.9 11.9 %all_to_all.87 = bf16[8,8,3584]{2,1,0:T(8,128)(2,1)S(1)} all-to-all(bf16[8,8,3584]{2,1,0:T(8,128)(2,1)} %reduce_sum.98), channel_id=1, replica_groups=mesh['batch'=4,'tensor_0'=4,'tensor_1'=2,'latent'=4] {'tensor_0','tensor..., dimensions={0} | all-to-all | bytes 917504 | tf_op jit(solution)/shard_map/all_to_all | solution.py:50
  131.9 11.1 %all_to_all.88 = bf16[8,8,3584]{2,1,0:T(8,128)(2,1)S(1)} all-to-all(bf16[8,8,3584]{2,1,0:T(8,128)(2,1)S(1)} %broadcast_in_dim.11), channel_id=1, replica_groups=mesh['batch'=4,'tensor_0'=4,'tensor_1'=2,'latent'=4] {'tensor_0','tensor..., dimensions={0} | all-to-all | bytes 917504 | tf_op jit(solution)/shard_map/all_to_all | solution.py:18
  148.2 17.5 %all-to-all-done.4 = bf16[4,8,8,3584]{3,2,1,0:T(8,128)(2,1)S(1)} async-done(((bf16[4,8,8,3584]{3,2,1,0:T(8,128)(2,1)}), bf16[4,8,8,3584]{3,2,1,0:T(8,128)(2,1)S(1)}, u32[]{:S(2)}, u32[]{:S(2)}) %all-to-all-start.4) | async-done | bytes 1835040 | tf_op jit(solution)/shard_map/all_to_all | solution.py:18
  168.0 5.1 copy.54
  190.1 29.4 %reduce-scatter.4.cloned.1.call-done = bf16[8,256,112]{1,2,0:T(8,128)(2,1)} async-done(((bf16[32,256,112]{1,2,0:T(8,128)(2,1)}), bf16[8,256,112]{1,2,0:T(8,128)(2,1)}) %reduce-scatter.4.cloned.1.call-update) | async-done | bytes 458768 | tf_op jit(solution)/shard_map/reduce_scatter | solution.py:66
  219.6 21.8 %reduce-scatter.6.cloned.1.call-done = bf16[2,256,112]{1,2,0:T(8,128)(2,1)} async-done(((bf16[8,256,112]{1,2,0:T(8,128)(2,1)}), bf16[2,256,112]{1,2,0:T(8,128)(2,1)}) %reduce-scatter.6.cloned.1.call-update) | async-done | bytes 114704 | tf_op jit(solution)/shard_map/reduce_scatter | solution.py:66
  241.4 17.6 %reduce-scatter.8.cloned.1.call-done = bf16[1,256,112]{1,2,0:T(8,128)(2,1)} async-done(((bf16[2,256,112]{1,2,0:T(8,128)(2,1)}), bf16[1,256,112]{1,2,0:T(8,128)(2,1)}) %reduce-scatter.8.cloned.1.call-update) | async-done | bytes 57360 | tf_op jit(solution)/shard_map/reduce_scatter | solution.py:66
  260.5 7.0 %all-to-all-start.5 = ((f32[32,1,256]{2,1,0:T(1,128)}), f32[32,1,256]{2,1,0:T(1,128)S(1)}, u32[]{:S(2)}, u32[]{:S(2)}) async-start(f32[32,1,256]{2,1,0:T(1,128)} %broadcast_in_dim.13), calls=%async_computation.8 | async-start | bytes 65536 | tf_op jit(solution)/shard_map/all_to_all | solution.py:18
  268.3 8.0 %all-to-all-done.5 = f32[32,1,256]{2,1,0:T(1,128)S(1)} async-done(((f32[32,1,256]{2,1,0:T(1,128)}), f32[32,1,256]{2,1,0:T(1,128)S(1)}, u32[]{:S(2)}, u32[]{:S(2)}) %all-to-all-start.5) | async-done | bytes 32800 | tf_op jit(solution)/shard_map/all_to_all | solution.py:18
  277.4 12.1 %all_to_all.89 = f32[32,1,256]{2,1,0:T(1,128)S(1)} all-to-all(f32[32,1,256]{2,1,0:T(1,128)S(1)} %broadcast_in_dim.14), channel_id=1, replica_groups=mesh['batch'=4,'tensor_0'=4,'tensor_1'=2,'latent'=4] {'tensor_0','tensor..., dimensions={0} | all-to-all | bytes 65536 | tf_op jit(solution)/shard_map/all_to_all | solution.py:18
  290.7 26.4 %all_to_all.90 = bf16[32,256,112]{1,2,0:T(8,128)(2,1)S(1)} all-to-all(bf16[32,256,112]{1,2,0:T(8,128)(2,1)S(1)} %stack.2), channel_id=1, replica_groups=mesh['batch'=4,'tensor_0'=4,'tensor_1'=2,'latent'=4] {'tensor_0','tensor..., dimensions={0} | all-to-all | bytes 3670016 | tf_op jit(solution)/shard_map/all_to_all | solution.py:144
  322.9 7.4 %all-to-all-start.8 = ((bf16[32,256,112]{1,2,0:T(8,128)(2,1)}), bf16[32,256,112]{1,2,0:T(8,128)(2,1)S(1)}, u32[]{:S(2)}, u32[]{:S(2)}) async-start(bf16[32,256,112]{1,2,0:T(8,128)(2,1)} %bitcast.18), calls=%async_computation.11 | async-start | bytes 3670016 | tf_op jit(solution)/shard_map/all_to_all | solution.py:42
  330.5 23.4 %all-to-all-done.8 = bf16[32,256,112]{1,2,0:T(8,128)(2,1)S(1)} async-done(((bf16[32,256,112]{1,2,0:T(8,128)(2,1)}), bf16[32,256,112]{1,2,0:T(8,128)(2,1)S(1)}, u32[]{:S(2)}, u32[]{:S(2)}) %all-to-all-start.8) | async-done | bytes 1835040 | tf_op jit(solution)/shard_map/all_to_all | solution.py:42
  355.2 15.6 %all_to_all.91 = f32[32,1,256]{2,1,0:T(1,128)S(1)} all-to-all(f32[32,1,256]{2,1,0:T(1,128)S(1)} %broadcast_in_dim.15), channel_id=1, replica_groups=mesh['batch'=4,'tensor_0'=4,'tensor_1'=2,'latent'=4] {'tensor_0','tensor..., dimensions={0} | all-to-all | bytes 65536 | tf_op jit(solution)/shard_map/all_to_all | solution.py:18
  372.5 65.9 %all-gather.6.cloned.1.call-done = bf16[256,3584]{0,1:T(8,128)(2,1)} async-done(((bf16[256,112]{0,1:T(8,128)(2,1)}), bf16[256,3584]{0,1:T(8,128)(2,1)}) %all-gather.6.cloned.1.call-update) | async-done | bytes 1835024 | tf_op jit(solution)/shard_map/all_gather | solution.py:163
  438.4 5.8 %fusion.11 = bf16[256,1024]{1,0:T(8,128)(2,1)S(1)} fusion(bf16[256,3584]{0,1:T(8,128)(2,1)} %all-gather.6.cloned.1.call-done, bf16[1024,3584]{1,0:T(8,128)(2,1)} %param.15, f32[256,1024]{1,0:T(8,128)S(1)} %copy-done.14), kind=kOutput, calls=%fused_computation.18 | convolution fusion | flops 1879834624 | bytes 10747904 | tf_op jit(solution)/shard_map/dot_general | solution.py:164
  446.1 44.0 %all_to_all.92 = bf16[256,4,896]{0,2,1:T(8,128)(2,1)} all-to-all(bf16[256,4,896]{0,2,1:T(8,128)(2,1)S(1)} %bitcast.57), channel_id=1, replica_groups=mesh['batch'=4,'tensor_0'=4,'tensor_1'=2,'latent'=4] {'batch'}, dimensions={1} | all-to-all | bytes 3670016 | tf_op jit(solution)/shard_map/all_to_all | solution.py:169
  490.1 5.0 all-to-all-start.10
  498.7 28.5 %all-to-all-done.10 = bf16[256,4,896]{0,2,1:T(8,128)(2,1)S(1)} async-done(((bf16[256,4,896]{0,2,1:T(8,128)(2,1)}), bf16[256,4,896]{0,2,1:T(8,128)(2,1)S(1)}, u32[]{:S(2)}, u32[]{:S(2)}) %all-to-all-start.10) | async-done | bytes 1835040 | tf_op jit(solution)/shard_map/all_to_all | solution.py:170
  529.6 5.9 %fusion.8 = bf16[1024,896]{1,0:T(8,128)(2,1)} fusion(bf16[1024,896]{1,0:T(8,128)(2,1)} %bitcast.66, bf16[1024,2048]{1,0:T(8,128)(2,1)} %all-gather.8.cloned.1.call-done), kind=kOutput, calls=%fused_computation.15 | convolution fusion | flops 1879965696 | bytes 5767168 | tf_op jit(solution)/shard_map/dot_general | solution.py:176
  (100 shorter events, 53.7 us)
Async XLA Ops:
  7.2 176.6 %copy-start = (bf16[224,3584]{1,0:T(8,128)(2,1)S(1)}, bf16[224,3584]{1,0:T(8,128)(2,1)}, u32[]{:S(2)}) copy-start(bf16[224,3584]{1,0:T(8,128)(2,1)} %param.21) | copy-start | bytes 4816900
  7.2 75.8 %all-gather.4.cloned.1.call-start = ((), (), s32[]{:S(2)}) async-start(), calls=%async_computation.14 | async-start | bytes 1892352 | tf_op jit(solution)/shard_map/all_gather | solution.py:113
  89.7 5.4 copy-start.9
  144.4 3.8 copy-start.17
  144.4 3.8 copy-start.18
  144.4 21.3 %all-to-all-start.4 = ((bf16[4,8,8,3584]{3,2,1,0:T(8,128)(2,1)}), bf16[4,8,8,3584]{3,2,1,0:T(8,128)(2,1)S(1)}, u32[]{:S(2)}, u32[]{:S(2)}) async-start(bf16[4,8,8,3584]{3,2,1,0:T(8,128)(2,1)} %broadcast_in_dim.12), calls=%async_computation.4 | async-start | bytes 3670016 | tf_op jit(solution)/shard_map/all_to_all | solution.py:18
  148.2 71.4 %reduce-scatter.4.cloned.1.call-start = ((), (), s32[]{:S(2)}) async-start(), calls=%async_computation.15 | async-start | bytes 2293760 | tf_op jit(solution)/shard_map/reduce_scatter | solution.py:66
  178.2 3.6 copy-start.2
  178.2 4.1 copy-start.5
  190.0 86.3 %copy-start.16 = (bf16[256,112]{0,1:T(8,128)(2,1)S(1)}, bf16[256,112]{0,1:T(8,128)(2,1)}, u32[]{:S(2)}) copy-start(bf16[256,112]{0,1:T(8,128)(2,1)} %param.12) | copy-start | bytes 172036
  190.1 51.3 %reduce-scatter.6.cloned.1.call-start = ((), (), s32[]{:S(2)}) async-start(), calls=%async_computation.16 | async-start | bytes 573440 | tf_op jit(solution)/shard_map/reduce_scatter | solution.py:66
  219.6 39.5 %reduce-scatter.8.cloned.1.call-start = ((), (), s32[]{:S(2)}) async-start(), calls=%async_computation.17 | async-start | bytes 172032 | tf_op jit(solution)/shard_map/reduce_scatter | solution.py:66
  260.5 15.7 %all-to-all-start.5 = ((f32[32,1,256]{2,1,0:T(1,128)}), f32[32,1,256]{2,1,0:T(1,128)S(1)}, u32[]{:S(2)}, u32[]{:S(2)}) async-start(f32[32,1,256]{2,1,0:T(1,128)} %broadcast_in_dim.13), calls=%async_computation.8 | async-start | bytes 65536 | tf_op jit(solution)/shard_map/all_to_all | solution.py:18
  322.9 31.0 %all-to-all-start.8 = ((bf16[32,256,112]{1,2,0:T(8,128)(2,1)}), bf16[32,256,112]{1,2,0:T(8,128)(2,1)S(1)}, u32[]{:S(2)}, u32[]{:S(2)}) async-start(bf16[32,256,112]{1,2,0:T(8,128)(2,1)} %bitcast.18), calls=%async_computation.11 | async-start | bytes 3670016 | tf_op jit(solution)/shard_map/all_to_all | solution.py:42
  330.3 40.5 %copy-start.15 = (bf16[1,256,112]{1,2,0:T(8,128)(2,1)S(1)}, bf16[1,256,112]{1,2,0:T(8,128)(2,1)}, u32[]{:S(2)}) copy-start(bf16[1,256,112]{1,2,0:T(8,128)(2,1)} %reduce-scatter.8.cloned.1.call-done) | copy-start | bytes 172036
  330.3 108.1 %copy-start.14 = (f32[256,1024]{1,0:T(8,128)S(1)}, f32[256,1024]{1,0:T(8,128)}, u32[]{:S(2)}) copy-start(f32[256,1024]{1,0:T(8,128)} %get-tuple-element.5) | copy-start | bytes 3145732
  330.4 108.1 %all-gather.6.cloned.1.call-start = ((), (), s32[]{:S(2)}) async-start(), calls=%async_computation.18 | async-start | bytes 1892352 | tf_op jit(solution)/shard_map/all_gather | solution.py:163
  372.5 157.1 %all-gather.8.cloned.1.call-start = ((), (), s32[]{:S(2)}) async-start(), calls=%async_computation.19 | async-start | bytes 5242880 | tf_op jit(solution)/shard_map/all_gather | solution.py:81
  438.4 5.8 %copy-start.10 = (bf16[256,1024]{1,0:T(8,128)(2,1)S(1)}, bf16[256,1024]{1,0:T(8,128)(2,1)}, u32[]{:S(2)}) copy-start(bf16[256,1024]{1,0:T(8,128)(2,1)} %copy-done.9) | copy-start | bytes 1572868
  444.2 1.9 copy-start.3
  490.1 37.1 %all-to-all-start.10 = ((bf16[256,4,896]{0,2,1:T(8,128)(2,1)}), bf16[256,4,896]{0,2,1:T(8,128)(2,1)S(1)}, u32[]{:S(2)}, u32[]{:S(2)}) async-start(bf16[256,4,896]{0,2,1:T(8,128)(2,1)} %bitcast.64), calls=%async_computation.13 | async-start | bytes 3670016 | tf_op jit(solution)/shard_map/all_to_all | solution.py:170
  529.6 5.9 %copy-start.13 = (bf16[4,256,896]{2,1,0:T(8,128)(2,1)S(1)}, bf16[4,256,896]{2,1,0:T(8,128)(2,1)}, u32[]{:S(2)}) copy-start(bf16[4,256,896]{2,1,0:T(8,128)(2,1)} %copy.51) | copy-start | bytes 5505028
  529.6 5.9 %copy-start.19 = (bf16[1024,2048]{1,0:T(8,128)(2,1)S(1)}, bf16[1024,2048]{1,0:T(8,128)(2,1)}, u32[]{:S(2)}) copy-start(bf16[1024,2048]{1,0:T(8,128)(2,1)} %all-gather.8.cloned.1.call-done) | copy-start | bytes 12582916
  535.5 3.4 copy-start.1
  (6 other events, 7.2 us)
Sparse Core Ops, SparseCore 0:
  11.7 71.2 all-gather.3
  190.2 29.3 reduce-scatter.3
  222.0 19.3 reduce-scatter.5
  243.7 15.3 reduce-scatter.7
  372.6 65.7 all-gather.5
  445.5 72.1 all-gather.7
